TPU v7x, 128 devices: a whole 4x4x4 slice. The times are simulated.
128 devices in a mesh: row: 8 (over y, core), col: 16 (over x, z).
Axes of the slice: x: 4, y: 4, z: 4, core: 2. Of those that a mesh axis runs over, the one named last changes fastest.
Arguments:
- strip_columns: float32 [4096, 32, 256], P(('row', 'col')), may hold values from -0.0048828125 to 0.0048828125
- tile_columns: float32 [4096, 4, 32, 256], P(('row', 'col')), may hold values from -6 to 6
- barrier_weights: float32 [4096, 32], P(('row', 'col')), may hold values from 0.01 to 100
- column_counts: int32 [4096], P(('row', 'col')), may hold values from 1 to 32
- tile_lists: int32 [4096, 4], P(('row', 'col')), may hold values from 0 to 127, all different within a row; in each aligned block of 32 rows (0 to 31, 32 to 63, ...) at most 2 rows name the same one
Outputs:
- panel_factor: float32 [256, 256], replicated
- strip_update: float32 [256, 32768], P(None, ('row', 'col'))
Inputs may be any that keep to these rules, and one draw needn't show every extreme that they name: `tile_lists`: each block lists 4 different column tiles; among the 32 blocks of one device no tile is listed more than 2 times, and in some device one tile is listed exactly 2 times.
All inputs are finite; a program needn't handle non-finite values.
Results may differ from a plain program's by a relative error of at most 0.0001.
Values sent between devices are 32-bit elements; how exact they have to be, the bound alone decides.
A program may use at most 192 MiB of HBM per device.

v0:
```python
import jax
import jax.numpy as jnp
from jax import lax
from jax.sharding import PartitionSpec as P


def per_device(strip_columns, tile_columns, barrier_weights, column_counts, tile_lists):
    highest = lax.Precision.HIGHEST
    blocks, block_width, strip_rows = strip_columns.shape
    touched = tile_columns.shape[1]
    own_width = tile_columns.shape[3]
    devices = lax.axis_size(("row", "col"))
    live_mask = jnp.arange(block_width, dtype=jnp.int32)[None, :] < column_counts[:, None]
    live_weight = jnp.where(live_mask, barrier_weights, 0.0)
    scaled = strip_columns * live_weight[:, :, None]
    local_diagonal = lax.dot_general(
        scaled, strip_columns, (((0, 1), (0, 1)), ((), ())), precision=highest
    )
    diagonal_block = lax.psum(local_diagonal, ("row", "col"))
    item_count = blocks * touched
    capacity = max(2, 2 * item_count // devices)
    targets = tile_lists.reshape(item_count)
    one_hot = (targets[:, None] == jnp.arange(devices, dtype=jnp.int32)[None, :]).astype(jnp.int32)
    earlier = jnp.cumsum(one_hot, axis=0) - one_hot
    ranked = jnp.sum(earlier * one_hot, axis=1)
    slot_index = targets * capacity + ranked
    slot_item = (
        jnp.full((devices * capacity,), -1, jnp.int32)
        .at[slot_index]
        .set(jnp.arange(item_count, dtype=jnp.int32))
    )
    filled = slot_item >= 0
    picked = jnp.maximum(slot_item, 0)
    send_strip = scaled[picked // touched]
    send_tile = tile_columns.reshape(item_count, block_width, own_width)[picked]
    outgoing = jnp.where(
        filled[:, None, None], jnp.concatenate([send_strip, send_tile], axis=2), 0.0
    )
    incoming = lax.all_to_all(outgoing, ("row", "col"), split_axis=0, concat_axis=0, tiled=True)
    tile_sum = lax.dot_general(
        incoming[:, :, :strip_rows],
        incoming[:, :, strip_rows:],
        (((0, 1), (0, 1)), ((), ())),
        precision=highest,
    )
    panel_factor = jnp.linalg.cholesky(diagonal_block)
    strip_update = jax.scipy.linalg.solve_triangular(panel_factor, tile_sum, lower=True)
    return (panel_factor, strip_update)


def solution(mesh):
    return jax.shard_map(
        per_device,
        mesh=mesh,
        in_specs=(
            P(("row", "col"), None, None),
            P(("row", "col"), None, None, None),
            P(("row", "col"), None),
            P(("row", "col")),
            P(("row", "col"), None),
        ),
        out_specs=(P(), P(None, ("row", "col"))),
        check_vma=False,
    )
```

profile of v0, /device:TPU:1, one launch (start us, length us, event | category | flops | bytes accessed | tf_op | source)
XLA Modules:
  0.0 456.5 jit_solution(12866232470006165996)
XLA Ops:
  7.2 0.7 broadcast_multiply_fusion.2
  7.8 0.8 copy.22
  9.4 1.0 scatter_custom_fusion
  10.4 0.8 fusion.18
  11.2 6.6 %gather_fusion.1 = f32[256,32,256]{2,1,0:T(8,128)} fusion(f32[128,32,256]{2,1,0:T(8,128)} %bitcast.43, s32[1024]{0:T(1024)S(1)} %get-tuple-element.34), kind=kCustom, calls=%fused_computation.1 | custom fusion | bytes 16778240 | tf_op jit(solution)/shard_map/gather | solution.py:35
  18.0 4.3 gather_fusion
  22.3 11.6 %maximum_select_fusion = f32[256,32,512]{2,1,0:T(8,128)} fusion(f32[256,32,256]{2,1,0:T(8,128)} %gather_fusion.1, f32[256,32,256]{2,1,0:T(8,128)} %gather_fusion, pred[256]{0:T(512)(128)(4,1)S(1)} %broadcast_compare_fusion), kind=kLoop, calls=%fused_computation.5 | loop fusion | flops 8388608 | bytes 33554688 | tf_op jit(solution)/shard_map/jit(_where)/select_n | solution.py:36
  34.0 12.0 %all-to-all-start = ((f32[256,32,512]{2,1,0:T(8,128)}), f32[256,32,512]{2,1,0:T(8,128)}, u32[]{:S(2)}, u32[]{:S(2)}) async-start(f32[256,32,512]{2,1,0:T(8,128)} %maximum_select_fusion), calls=%async_computation | async-start | bytes 33554432 | tf_op jit(solution)/shard_map/all_to_all | solution.py:39
  46.0 0.4 all-reduce.3.cloned.1.call-start
  46.4 2.7 convolution_bitcast_fusion
  49.1 297.1 %all-reduce.3.cloned.1.call-done = f32[256,256]{0,1:T(8,128)} async-done(((f32[256,256]{0,1:T(8,128)}), f32[256,256]{0,1:T(8,128)}) %all-reduce.3.cloned.1.call-update) | async-done | bytes 262160 | tf_op jit(solution)/shard_map/psum | solution.py:19
  346.2 1.1 copy.20
  347.3 1.0 fusion.8
  348.3 11.7 %cholesky.51 = f32[128,128]{1,0:T(8,128)S(1)} custom-call(f32[128,128]{1,0:T(8,128)S(1)} %cholesky.121), custom_call_target="Cholesky" | custom-call | tf_op jit(solution)/shard_map/jit(cholesky)/cholesky | solution.py:46
  360.1 9.8 %custom-call.15 = f32[1,128,128]{1,2,0:T(8,128)S(1)} custom-call(f32[1,128,128]{2,1,0:T(8,128)S(1)} %get-tuple-element.27), custom_call_target="InvertDiagBlocksLowerTriangular" | custom-call | tf_op jit(solution)/shard_map/jit(cholesky)/cholesky | solution.py:46
  369.9 0.2 constant_dynamic-update-slice_fusion.1
  370.1 0.3 convolution_subtract_fusion.1
  370.4 22.5 %cholesky.107 = f32[128,128]{1,0:T(8,128)S(1)} custom-call(f32[128,128]{1,0:T(8,128)S(1)} %convolution_subtract_fusion.1), custom_call_target="Cholesky" | custom-call | tf_op jit(solution)/shard_map/jit(cholesky)/cholesky | solution.py:46
  392.9 0.6 compare_reduce_fusion
  394.9 0.7 fusion.9
  395.7 4.0 while.1
  395.7 0.6 fusion.30
  396.3 1.4 bitcast_dynamic-update-slice_fusion.2
  397.7 0.6 fusion.30
  398.3 1.4 bitcast_dynamic-update-slice_fusion.2
  399.7 19.7 %custom-call.16 = f32[2,128,128]{1,2,0:T(8,128)S(1)} custom-call(f32[2,128,128]{2,1,0:T(8,128)S(1)} %get-tuple-element.9), custom_call_target="InvertDiagBlocksLowerTriangular" | custom-call | tf_op jit(solution)/shard_map/jit(_solve_triangular)/triangular_solve | solution.py:47
  419.4 6.8 %fusion.23 = (f32[256,32,256]{2,1,0:T(8,128)S(1)}, f32[256,32,256]{2,1,0:T(8,128)S(1)}) fusion(f32[256,32,512]{2,1,0:T(8,128)} %all-to-all-done), kind=kLoop, calls=%fused_computation.57 | loop fusion | bytes 33554432 | tf_op jit(solution)/shard_map/slice | solution.py:41
  426.2 21.6 %fusion.3 = f32[256,256]{1,0:T(8,128)S(1)} fusion(f32[256,32,256]{2,1,0:T(8,128)S(1)} %get-tuple-element.23, f32[256,32,256]{2,1,0:T(8,128)S(1)} %get-tuple-element.22), kind=kOutput, calls=%fused_computation.9 | convolution fusion | flops 6442450944 | bytes 17039360 | tf_op jit(solution)/shard_map/dot_general | solution.py:40
  447.8 0.3 fusion.10
  448.1 0.3 convolution_subtract_fusion
  448.4 0.3 fusion.13
  448.7 0.7 pad_maximum_fusion
  (25 shorter events, 1.2 us)
Async XLA Ops:
  11.2 6.6 %copy-start = (f32[32,32,256]{2,1,0:T(8,128)S(1)}, f32[32,32,256]{2,1,0:T(8,128)}, u32[]{:S(2)}) copy-start(f32[32,32,256]{2,1,0:T(8,128)} %param.5) | copy-start | bytes 3145732
  34.0 385.4 %all-to-all-start = ((f32[256,32,512]{2,1,0:T(8,128)}), f32[256,32,512]{2,1,0:T(8,128)}, u32[]{:S(2)}, u32[]{:S(2)}) async-start(f32[256,32,512]{2,1,0:T(8,128)} %maximum_select_fusion), calls=%async_computation | async-start | bytes 33554432 | tf_op jit(solution)/shard_map/all_to_all | solution.py:39
  46.0 300.3 %all-reduce.3.cloned.1.call-start = ((), (), s32[]{:S(2)}) async-start(), calls=%async_computation.1 | async-start | bytes 524288 | tf_op jit(solution)/shard_map/psum | solution.py:19
Sparse Core Ops, SparseCore 0:
  52.1 294.0 all-reduce.2
where the time goes:
time: 460 us; the launch traced here: 456 us
  waiting for transfers between devices  297 us (65%)
  other arithmetic  80.6 us (18%)
  matrix products  25.6 us (6%)
  local copies, waits for them, and re-layouts  24.9 us (5%)
  between operations  15.8 us (3%)
  starting transfers between devices  12.4 us (3%)
    psum x1, waiting for transfers between devices, per_device(): diagonal_block = lax.psum(local_diagonal, ('row', 'col'))  297 us
    another operation x6, other arithmetic, per_device(): panel_factor = jnp.linalg.cholesky(diagonal_block)  44.7 us
    dot_general x1, matrix products, per_device(): lax.dot_general(incoming[:, :, :strip_rows], incoming[:, :, strip_rows:],...  21.6 us
    another operation x4, other arithmetic, per_device(): jax.scipy.linalg.solve_triangular(panel_factor, tile_sum, lower=True)  21.1 us
    all_to_all x1, starting transfers between devices, per_device(): lax.all_to_all(outgoing, ('row', 'col'), split_axis=0, concat_axis=0, til...  12 us
    select_n x1, other arithmetic, per_device(): jnp.where(filled[:, None, None], jnp.concatenate([send_strip, send_tile],...  11.6 us
  transfers between devices with their start and end apart: 2, of which 1 were waited for; matrix products, arithmetic and copies ran while one was open for 16% of the time, Pallas kernels for 0%

commit v1 on v0

--- a/solution.py
+++ b/solution.py
@@ -16,7 +16,8 @@
     local_diagonal = lax.dot_general(
         scaled, strip_columns, (((0, 1), (0, 1)), ((), ())), precision=highest
     )
-    diagonal_block = lax.psum(local_diagonal, ("row", "col"))
+    shards = lax.all_gather(local_diagonal, ("row", "col"), axis=0, tiled=False)
+    diagonal_block = shards.sum(axis=0)
     item_count = blocks * touched
     capacity = max(2, 2 * item_count // devices)
     targets = tile_lists.reshape(item_count)

time: 460 us -> 442 us (0.961); the launches traced: 456 us -> 433 us
  waiting for transfers between devices: 297 us -> 273 us
    psum x1 -> x0, waiting for transfers between devices: 297 us -> none  [per_device(): diagonal_block = lax.psum(local_diagonal, ('row', 'col'))]
    all_to_all x1, waiting for transfers between devices: 0.01 us -> 273 us  [per_device(): lax.all_to_all(outgoing, ('row', 'col'), split_axis=0, concat_axis=0, til...]
    reduce_sum x0 -> x1, other arithmetic: none -> 12.2 us  [per_device(): diagonal_block = shards.sum(axis=0)]
    another operation x6, other arithmetic: 44.7 us -> 33.9 us  [per_device(): panel_factor = jnp.linalg.cholesky(diagonal_block)]
  transfers between devices with their start and end apart: 2 -> 2, of which waited for: 1 -> 1; matrix products, arithmetic and copies ran while one was open for 16% -> 13% of each run, Pallas kernels for 0% -> 0%
where the time goes in v1:
time: 442 us; the launch traced here: 433 us
  waiting for transfers between devices  273 us (62%)
  other arithmetic  81.4 us (18%)
  matrix products  27.2 us (6%)
  local copies, waits for them, and re-layouts  24.5 us (6%)
  between operations  15.8 us (4%)
  starting transfers between devices  12 us (3%)
    all_to_all x1, waiting for transfers between devices, per_device(): lax.all_to_all(outgoing, ('row', 'col'), split_axis=0, concat_axis=0, til...  273 us
    another operation x6, other arithmetic, per_device(): panel_factor = jnp.linalg.cholesky(diagonal_block)  33.9 us
    dot_general x1, matrix products, per_device(): lax.dot_general(incoming[:, :, :strip_rows], incoming[:, :, strip_rows:],...  21.6 us
    another operation x4, other arithmetic, per_device(): jax.scipy.linalg.solve_triangular(panel_factor, tile_sum, lower=True)  21.4 us
    reduce_sum x1, other arithmetic, per_device(): diagonal_block = shards.sum(axis=0)  12.2 us
    all_to_all x1, starting transfers between devices, per_device(): lax.all_to_all(outgoing, ('row', 'col'), split_axis=0, concat_axis=0, til...  12 us
    select_n x1, other arithmetic, per_device(): jnp.where(filled[:, None, None], jnp.concatenate([send_strip, send_tile],...  11.7 us
  transfers between devices with their start and end apart: 2, of which 1 were waited for; matrix products, arithmetic and copies ran while one was open for 13% of the time, Pallas kernels for 0%

profile of v1, /device:TPU:1, one launch (start us, length us, event | category | flops | bytes accessed | tf_op | source)
XLA Modules:
  0.0 433.5 jit_solution(64877964339892035)
XLA Ops:
  7.2 0.8 fusion.18
  8.0 4.2 convolution_bitcast_fusion
  12.3 0.8 copy.19
  13.0 0.7 broadcast_multiply_fusion.2
  14.1 0.2 reduce_window_sum.11
  14.5 1.0 scatter_custom_fusion
  15.5 6.6 %gather_fusion.1 = f32[256,32,256]{2,1,0:T(8,128)} fusion(f32[128,32,256]{2,1,0:T(8,128)} %bitcast.45, s32[1024]{0:T(1024)S(1)} %get-tuple-element.34), kind=kCustom, calls=%fused_computation.1 | custom fusion | bytes 16778240 | tf_op jit(solution)/shard_map/gather | solution.py:36
  22.1 0.2 broadcast_multiply_fusion
  22.3 4.3 gather_fusion
  26.6 11.7 %maximum_select_fusion = f32[256,32,512]{2,1,0:T(8,128)} fusion(f32[256,32,256]{2,1,0:T(8,128)} %gather_fusion.1, f32[256,32,256]{2,1,0:T(8,128)} %gather_fusion, pred[256]{0:T(512)(128)(4,1)S(1)} %broadcast_compare_fusion), kind=kLoop, calls=%fused_computation.5 | loop fusion | flops 8388608 | bytes 33554688 | tf_op jit(solution)/shard_map/jit(_where)/select_n | solution.py:37
  38.4 12.0 %all-to-all-start = ((f32[256,32,512]{2,1,0:T(8,128)}), f32[256,32,512]{2,1,0:T(8,128)}, u32[]{:S(2)}, u32[]{:S(2)}) async-start(f32[256,32,512]{2,1,0:T(8,128)} %maximum_select_fusion), calls=%async_computation | async-start | bytes 33554432 | tf_op jit(solution)/shard_map/all_to_all | solution.py:40
  50.4 272.5 %all-to-all-done = f32[256,32,512]{2,1,0:T(8,128)} async-done(((f32[256,32,512]{2,1,0:T(8,128)}), f32[256,32,512]{2,1,0:T(8,128)}, u32[]{:S(2)}, u32[]{:S(2)}) %all-to-all-start) | async-done | bytes 16777248 | tf_op jit(solution)/shard_map/all_to_all | solution.py:40
  322.9 7.3 %fusion.23 = (f32[256,32,256]{2,1,0:T(8,128)S(1)}, f32[256,32,256]{2,1,0:T(8,128)S(1)}) fusion(f32[256,32,512]{2,1,0:T(8,128)} %all-to-all-done), kind=kLoop, calls=%fused_computation.57 | loop fusion | bytes 33554432 | tf_op jit(solution)/shard_map/slice | solution.py:42
  330.2 21.6 %fusion.3 = f32[256,256]{1,0:T(8,128)S(1)} fusion(f32[256,32,256]{2,1,0:T(8,128)S(1)} %get-tuple-element.23, f32[256,32,256]{2,1,0:T(8,128)S(1)} %get-tuple-element.22), kind=kOutput, calls=%fused_computation.9 | convolution fusion | flops 6442450944 | bytes 17039360 | tf_op jit(solution)/shard_map/dot_general | solution.py:41
  351.8 12.2 %reduce_sum.20 = f32[256,256]{1,0:T(8,128)S(1)} reduce(f32[128,256,256]{2,1,0:T(8,128)} %bitcast.44, f32[]{:T(128)} %constant.101.clone.1), dimensions={0}, to_apply=%region_0.1 | reduce | flops 8323072 | bytes 33816580 | tf_op jit(solution)/shard_map/reduce_sum | solution.py:20
  364.2 11.7 %cholesky.51 = f32[128,128]{1,0:T(8,128)S(1)} custom-call(f32[128,128]{1,0:T(8,128)S(1)} %cholesky.121), custom_call_target="Cholesky" | custom-call | tf_op jit(solution)/shard_map/jit(cholesky)/cholesky | solution.py:47
  375.9 9.8 %custom-call.15 = f32[1,128,128]{1,2,0:T(8,128)S(1)} custom-call(f32[1,128,128]{2,1,0:T(8,128)S(1)} %get-tuple-element.27), custom_call_target="InvertDiagBlocksLowerTriangular" | custom-call | tf_op jit(solution)/shard_map/jit(cholesky)/cholesky | solution.py:47
  385.7 0.2 constant_dynamic-update-slice_fusion.1
  386.0 0.3 convolution_subtract_fusion.1
  386.2 11.7 %cholesky.107 = f32[128,128]{1,0:T(8,128)S(1)} custom-call(f32[128,128]{1,0:T(8,128)S(1)} %convolution_subtract_fusion.1), custom_call_target="Cholesky" | custom-call | tf_op jit(solution)/shard_map/jit(cholesky)/cholesky | solution.py:47
  398.0 0.6 compare_reduce_fusion
  399.9 0.7 fusion.9
  400.7 4.1 while.1
  400.7 0.6 fusion.30
  401.3 1.4 bitcast_dynamic-update-slice_fusion.2
  402.8 0.6 fusion.30
  403.4 1.4 bitcast_dynamic-update-slice_fusion.2
  404.8 19.9 %custom-call.16 = f32[2,128,128]{1,2,0:T(8,128)S(1)} custom-call(f32[2,128,128]{2,1,0:T(8,128)S(1)} %get-tuple-element.9), custom_call_target="InvertDiagBlocksLowerTriangular" | custom-call | tf_op jit(solution)/shard_map/jit(_solve_triangular)/triangular_solve | solution.py:48
  424.8 0.3 fusion.10
  425.1 0.3 convolution_subtract_fusion
  425.3 0.3 fusion.13
  425.7 0.7 pad_maximum_fusion
  (26 shorter events, 1.0 us)
Async XLA Ops:
  7.2 344.6 %all-gather.3.cloned.1.call-start = ((), (), s32[]{:S(2)}) async-start(), calls=%async_computation.1 | async-start | bytes 33816576 | tf_op jit(solution)/shard_map/all_gather | solution.py:19
  15.5 6.6 %copy-start = (f32[32,32,256]{2,1,0:T(8,128)S(1)}, f32[32,32,256]{2,1,0:T(8,128)}, u32[]{:S(2)}) copy-start(f32[32,32,256]{2,1,0:T(8,128)} %param.5) | copy-start | bytes 3145732
  38.4 284.5 %all-to-all-start = ((f32[256,32,512]{2,1,0:T(8,128)}), f32[256,32,512]{2,1,0:T(8,128)}, u32[]{:S(2)}, u32[]{:S(2)}) async-start(f32[256,32,512]{2,1,0:T(8,128)} %maximum_select_fusion), calls=%async_computation | async-start | bytes 33554432 | tf_op jit(solution)/shard_map/all_to_all | solution.py:40
Sparse Core Ops, SparseCore 0:
  12.4 302.9 all-gather.2

commit v2 on v0

--- a/solution.py
+++ b/solution.py
@@ -2,6 +2,11 @@
 import jax.numpy as jnp
 from jax import lax
 from jax.sharding import PartitionSpec as P
+
+
+def axis_by_axis(x, first, second):
+    partial = lax.psum(x, first)
+    return lax.psum(partial, second)
 
 
 def per_device(strip_columns, tile_columns, barrier_weights, column_counts, tile_lists):
@@ -16,7 +21,7 @@
     local_diagonal = lax.dot_general(
         scaled, strip_columns, (((0, 1), (0, 1)), ((), ())), precision=highest
     )
-    diagonal_block = lax.psum(local_diagonal, ("row", "col"))
+    diagonal_block = axis_by_axis(local_diagonal, "row", "col")
     item_count = blocks * touched
     capacity = max(2, 2 * item_count // devices)
     targets = tile_lists.reshape(item_count)

time: 460 us -> 451 us (0.980)
  other arithmetic: 80.6 us -> 69.9 us
    another operation x6, other arithmetic: 44.7 us -> 33.9 us  [per_device(): panel_factor = jnp.linalg.cholesky(diagonal_block)]
    psum x1 -> x2, waiting for transfers between devices: 297 us -> 297 us  [the longest x1 165 us: axis_by_axis(): partial = lax.psum(x, first)]
  transfers between devices with their start and end apart: 2 -> 3, of which waited for: 1 -> 2; matrix products, arithmetic and copies ran while one was open for 16% -> 14% of each run, Pallas kernels for 0% -> 0%
where the time goes in v2:
time: 451 us; the launch traced here: 446 us
  waiting for transfers between devices  297 us (66%)
  other arithmetic  69.9 us (15%)
  matrix products  25.7 us (6%)
  local copies, waits for them, and re-layouts  25.1 us (6%)
  between operations  15.8 us (4%)
  starting transfers between devices  12.5 us (3%)
    psum x1, waiting for transfers between devices, axis_by_axis(): partial = lax.psum(x, first)  165 us
    psum x1, waiting for transfers between devices, axis_by_axis(): return lax.psum(partial, second)  132 us
    another operation x6, other arithmetic, per_device(): panel_factor = jnp.linalg.cholesky(diagonal_block)  33.9 us
    dot_general x1, matrix products, per_device(): lax.dot_general(incoming[:, :, :strip_rows], incoming[:, :, strip_rows:],...  21.6 us
    another operation x4, other arithmetic, per_device(): jax.scipy.linalg.solve_triangular(panel_factor, tile_sum, lower=True)  21.1 us
    all_to_all x1, starting transfers between devices, per_device(): lax.all_to_all(outgoing, ('row', 'col'), split_axis=0, concat_axis=0, til...  12 us
    select_n x1, other arithmetic, per_device(): jnp.where(filled[:, None, None], jnp.concatenate([send_strip, send_tile],...  11.6 us
  transfers between devices with their start and end apart: 3, of which 2 were waited for; matrix products, arithmetic and copies ran while one was open for 14% of the time, Pallas kernels for 0%

profile of v2, /device:TPU:1, one launch (start us, length us, event | category | flops | bytes accessed | tf_op | source)
XLA Modules:
  0.0 446.0 jit_solution(14497599377031017640)
XLA Ops:
  7.2 0.7 broadcast_multiply_fusion.2
  7.8 0.8 copy.22
  9.4 1.0 scatter_custom_fusion
  10.4 0.8 fusion.18
  11.2 6.6 %gather_fusion.1 = f32[256,32,256]{2,1,0:T(8,128)} fusion(f32[128,32,256]{2,1,0:T(8,128)} %bitcast.43, s32[1024]{0:T(1024)S(1)} %get-tuple-element.34), kind=kCustom, calls=%fused_computation.1 | custom fusion | bytes 16778240 | tf_op jit(solution)/shard_map/gather | solution.py:40
  18.0 4.3 gather_fusion
  22.3 11.6 %maximum_select_fusion = f32[256,32,512]{2,1,0:T(8,128)} fusion(f32[256,32,256]{2,1,0:T(8,128)} %gather_fusion.1, f32[256,32,256]{2,1,0:T(8,128)} %gather_fusion, pred[256]{0:T(512)(128)(4,1)S(1)} %broadcast_compare_fusion), kind=kLoop, calls=%fused_computation.5 | loop fusion | flops 8388608 | bytes 33554688 | tf_op jit(solution)/shard_map/jit(_where)/select_n | solution.py:41
  34.0 12.0 %all-to-all-start = ((f32[256,32,512]{2,1,0:T(8,128)}), f32[256,32,512]{2,1,0:T(8,128)}, u32[]{:S(2)}, u32[]{:S(2)}) async-start(f32[256,32,512]{2,1,0:T(8,128)} %maximum_select_fusion), calls=%async_computation | async-start | bytes 33554432 | tf_op jit(solution)/shard_map/all_to_all | solution.py:44
  46.0 2.7 convolution_bitcast_fusion
  48.7 0.5 all-reduce.6.cloned.1.call-start
  49.2 165.3 %all-reduce.4.cloned.1.call-done = f32[256,256]{0,1:T(8,128)} async-done(((f32[256,256]{0,1:T(8,128)}), f32[256,256]{0,1:T(8,128)}) %all-reduce.4.cloned.1.call-update) | async-done | bytes 262160 | tf_op jit(solution)/shard_map/psum | solution.py:8
  214.6 131.8 %all-reduce.6.cloned.1.call-done = f32[256,256]{0,1:T(8,128)} async-done(((f32[256,256]{0,1:T(8,128)}), f32[256,256]{0,1:T(8,128)}) %all-reduce.6.cloned.1.call-update) | async-done | bytes 262160 | tf_op jit(solution)/shard_map/psum | solution.py:9
  346.4 1.1 copy.20
  347.5 1.0 fusion.8
  348.5 11.7 %cholesky.51 = f32[128,128]{1,0:T(8,128)S(1)} custom-call(f32[128,128]{1,0:T(8,128)S(1)} %cholesky.121), custom_call_target="Cholesky" | custom-call | tf_op jit(solution)/shard_map/jit(cholesky)/cholesky | solution.py:51
  360.2 9.8 %custom-call.15 = f32[1,128,128]{1,2,0:T(8,128)S(1)} custom-call(f32[1,128,128]{2,1,0:T(8,128)S(1)} %get-tuple-element.27), custom_call_target="InvertDiagBlocksLowerTriangular" | custom-call | tf_op jit(solution)/shard_map/jit(cholesky)/cholesky | solution.py:51
  370.3 0.3 convolution_subtract_fusion.1
  370.5 11.7 %cholesky.107 = f32[128,128]{1,0:T(8,128)S(1)} custom-call(f32[128,128]{1,0:T(8,128)S(1)} %convolution_subtract_fusion.1), custom_call_target="Cholesky" | custom-call | tf_op jit(solution)/shard_map/jit(cholesky)/cholesky | solution.py:51
  382.3 0.6 compare_reduce_fusion
  384.2 0.7 fusion.9
  385.0 4.0 while.1
  385.1 0.6 fusion.30
  385.6 1.4 bitcast_dynamic-update-slice_fusion.2
  387.1 0.6 fusion.30
  387.7 1.4 bitcast_dynamic-update-slice_fusion.2
  389.1 19.7 %custom-call.16 = f32[2,128,128]{1,2,0:T(8,128)S(1)} custom-call(f32[2,128,128]{2,1,0:T(8,128)S(1)} %get-tuple-element.9), custom_call_target="InvertDiagBlocksLowerTriangular" | custom-call | tf_op jit(solution)/shard_map/jit(_solve_triangular)/triangular_solve | solution.py:52
  408.8 6.9 %fusion.23 = (f32[256,32,256]{2,1,0:T(8,128)S(1)}, f32[256,32,256]{2,1,0:T(8,128)S(1)}) fusion(f32[256,32,512]{2,1,0:T(8,128)} %all-to-all-done), kind=kLoop, calls=%fused_computation.57 | loop fusion | bytes 33554432 | tf_op jit(solution)/shard_map/slice | solution.py:46
  415.7 21.6 %fusion.3 = f32[256,256]{1,0:T(8,128)S(1)} fusion(f32[256,32,256]{2,1,0:T(8,128)S(1)} %get-tuple-element.23, f32[256,32,256]{2,1,0:T(8,128)S(1)} %get-tuple-element.22), kind=kOutput, calls=%fused_computation.9 | convolution fusion | flops 6442450944 | bytes 17039360 | tf_op jit(solution)/shard_map/dot_general | solution.py:45
  437.3 0.3 fusion.10
  437.7 0.3 convolution_subtract_fusion
  437.9 0.3 fusion.13
  438.2 0.7 pad_maximum_fusion
  (28 shorter events, 1.4 us)
Async XLA Ops:
  11.2 6.6 %copy-start = (f32[32,32,256]{2,1,0:T(8,128)S(1)}, f32[32,32,256]{2,1,0:T(8,128)}, u32[]{:S(2)}) copy-start(f32[32,32,256]{2,1,0:T(8,128)} %param.5) | copy-start | bytes 3145732
  34.0 374.8 %all-to-all-start = ((f32[256,32,512]{2,1,0:T(8,128)}), f32[256,32,512]{2,1,0:T(8,128)}, u32[]{:S(2)}, u32[]{:S(2)}) async-start(f32[256,32,512]{2,1,0:T(8,128)} %maximum_select_fusion), calls=%async_computation | async-start | bytes 33554432 | tf_op jit(solution)/shard_map/all_to_all | solution.py:44
  46.0 168.6 %all-reduce.4.cloned.1.call-start = ((), (), s32[]{:S(2)}) async-start(), calls=%async_computation.1 | async-start | bytes 524288 | tf_op jit(solution)/shard_map/psum | solution.py:8
  48.7 297.7 %all-reduce.6.cloned.1.call-start = ((), (), s32[]{:S(2)}) async-start(), calls=%async_computation.2 | async-start | bytes 524288 | tf_op jit(solution)/shard_map/psum | solution.py:9
Sparse Core Ops, SparseCore 0:
  49.7 164.8 all-reduce.3
  218.1 128.2 all-reduce.5
